TPU v7x, 32 devices: a whole 2x2x4 slice. The times are simulated.
32 devices in a mesh: keys: 8 (over z, x), heads: 4 (over y, core).
Axes of the slice: x: 2, y: 2, z: 4, core: 2. Of those that a mesh axis runs over, the one named last changes fastest.
Arguments:
- queries: bfloat16 [64, 64, 128], P(None, 'heads'), may hold values from -128 to 128
- keys: bfloat16 [131072, 8, 128], P('keys', 'heads'), may hold values from -4 to 4
- values: bfloat16 [131072, 8, 128], P('keys', 'heads'), may hold values from -6 to 6
- out_weight: bfloat16 [8192, 8192], P('heads', 'keys'), may hold values from -0.0625 to 0.0625
- probe: bfloat16 [8192], P('keys'), may hold values from -6 to 6
- knocked: int32 [64, 16], replicated, may hold values from 0 to 31
Outputs:
- readout: float32 [64, 32], P(None, 'keys')
- picked: float32 [64, 16], replicated
All inputs are finite; a program needn't handle non-finite values.
Results may differ from a plain program's by a relative error of at most 0.0003.
Values sent between devices are 32-bit elements; how exact they have to be, the bound alone decides.
A program may use at most 128 MiB of HBM per device.

v0:
```python
import jax
import jax.numpy as jnp
from jax import lax
from jax.sharding import PartitionSpec as P

BLOCK = 4096


NEG = -1e30


def entering(x, axis, combine, identity, reverse):
    size, position = (lax.axis_size(axis), lax.axis_index(axis))
    everything = jax.tree.map(lambda part: lax.all_gather(part, axis), x)
    start = jax.tree.map(
        lambda part, zero: jnp.broadcast_to(jnp.asarray(zero, part.dtype), part.shape), x, identity
    )

    def turn(k, before):
        at = size - 1 - k if reverse else k
        reached = at > position if reverse else at < position
        new = combine(before, jax.tree.map(lambda part: part[at], everything))
        return jax.tree.map(lambda a, b: jnp.where(reached, a, b), new, before)

    return lax.fori_loop(0, size, turn, start)


def stretch(factor, target):
    return factor.reshape(factor.shape + (1,) * (target.ndim - factor.ndim))


def combine(first, second):
    m1, s1, o1 = first
    m2, s2, o2 = second
    top = jnp.maximum(m1, m2)
    a = jnp.exp(m1 - top)
    b = jnp.exp(m2 - top)
    return (top, s1 * a + s2 * b, o1 * stretch(a, o1) + o2 * stretch(b, o2))


def body(queries, keys, values, out_weight, probe, knocked):
    nq, hq, hd = queries.shape
    kvh = keys.shape[1]
    group = hq // kvh
    nblk = keys.shape[0] // BLOCK
    lanes = lax.axis_size("keys")
    device = lax.axis_index("keys")
    context = keys.shape[0] * lanes
    direction = lax.psum(jnp.dot(out_weight, probe, preferred_element_type=jnp.float32), "keys")
    direction = direction.reshape(kvh, group, hd)
    grouped = queries.reshape(nq, kvh, group, hd)
    key_blocks = keys.reshape(nblk, BLOCK, kvh, hd)
    value_blocks = values.reshape(nblk, BLOCK, kvh, hd)
    query_pos = context - nq + jnp.arange(nq, dtype=jnp.int32)

    def block_state(inputs):
        kblk, vblk, local = inputs
        scores = jnp.einsum(
            "qgrd,kgd->qgrk", grouped, kblk, preferred_element_type=jnp.float32
        ) * hd ** (-0.5)
        key_pos = (device * nblk + local) * BLOCK + jnp.arange(BLOCK, dtype=jnp.int32)
        allowed = key_pos[None, :] <= query_pos[:, None]
        scores = jnp.where(allowed[:, None, None, :], scores, NEG)
        top = jnp.max(scores, axis=-1)
        weights = jnp.exp(scores - top[..., None])
        total = jnp.sum(weights, axis=-1)
        summed = jnp.einsum(
            "qgrk,kgd->qgrd", weights.astype(jnp.bfloat16), vblk, preferred_element_type=jnp.float32
        )
        summed = jnp.sum(summed * direction, axis=-1)
        return (top, total, summed)

    states = lax.map(block_state, (key_blocks, value_blocks, jnp.arange(nblk, dtype=jnp.int32)))
    empty = (
        jnp.full(states[0].shape[1:], NEG, jnp.float32),
        jnp.zeros(states[1].shape[1:], jnp.float32),
        jnp.zeros(states[2].shape[1:], jnp.float32),
    )

    def member(index):
        return (states[0][index], states[1][index], states[2][index])

    inner_before = [empty]
    for index in range(nblk - 1):
        inner_before.append(combine(inner_before[-1], member(index)))
    inner_after = [empty]
    for index in range(nblk - 1, 0, -1):
        inner_after.insert(0, combine(member(index), inner_after[0]))
    device_total = combine(inner_before[-1], member(nblk - 1))
    before = entering(device_total, "keys", combine, empty, False)
    after = entering(device_total, "keys", combine, empty, True)
    columns = []
    for index in range(nblk):
        state = combine(combine(before, inner_before[index]), combine(inner_after[index], after))
        top, total, summed = state
        columns.append(jnp.sum(summed / total, axis=(1, 2)))
    partial_read = jnp.stack(columns, axis=1)
    readout = lax.psum(partial_read, "heads")
    global_ids = device * nblk + jnp.arange(nblk, dtype=jnp.int32)
    matches = knocked[:, :, None] == global_ids[None, None, :]
    local_pick = jnp.sum(jnp.where(matches, readout[:, None, :], 0.0), axis=-1)
    picked = lax.psum(local_pick, "keys")
    return (readout, picked)


def solution(mesh):
    in_specs = (
        P(None, "heads", None),
        P("keys", "heads", None),
        P("keys", "heads", None),
        P("heads", "keys"),
        P("keys"),
        P(),
    )
    out_specs = (P(None, "keys"), P())
    return jax.shard_map(body, mesh=mesh, in_specs=in_specs, out_specs=out_specs, check_vma=False)
```

profile of v0, /device:TPU:0, one launch (start us, length us, event | category | flops | bytes accessed | tf_op | source)
XLA Modules:
  0.0 247.9 jit_solution(1460303861700542163)
XLA Ops:
  0.6 1.0 copy.26
  1.7 0.7 reshape.54
  2.4 3.4 %fusion.116 = f32[1,2048]{1,0:T(1,128)S(1)} fusion(bf16[2048,1024]{1,0:T(8,128)(2,1)} %param.15, bf16[1024,1]{0,1:T(2,128)(2,1)S(1)} %reshape.54), kind=kOutput, calls=%fused_computation.194 | convolution fusion | flops 4194304 | bytes 4204544 | tf_op jit(solution)/shard_map/dot_general | solution.py:49
  5.7 23.4 %psum.21 = f32[2048]{0:T(1024)S(1)} all-reduce(f32[2048]{0:T(1024)S(1)} %bitcast.455), channel_id=1, replica_groups=mesh['keys'=8,'heads'=4] {'keys'}, use_global_device_ids=true, to_apply=%region_0.0 | all-reduce | flops 2048 | bytes 16384 | tf_op jit(solution)/shard_map/psum | solution.py:49
  29.1 0.0 copy-start.1
  29.1 102.3 %while.55 = (s32[]{:T(128)}, f32[4,64,2,8]{1,3,2,0:T(8,128)S(1)}, f32[4,64,2,8]{1,3,2,0:T(8,128)S(1)}, f32[4,64,2,8]{1,3,2,0:T(8,128)S(1)}, s32[4]{0:T(128)S(1)}...) while((s32[]{:T(128)}, f32[4,64,2,8]{1,3,2,0:T(8,128)S(1)}, ...), condition=%wide.region_5.6_spmd.clone, body=%wide.region_1.5_spmd.clone.sunk | while | flops 2194146304 | bytes 131445448 | solution.py:73
  29.2 0.7 dynamic_slice.114
  30.5 0.2 broadcast_compare_fusion.2
  30.7 3.3 %constant_dynamic-slice_fusion.4 = bf16[1,4096,2,128]{3,2,1,0:T(2,128)(2,1)S(1)} fusion(bf16[4,4096,2,128]{3,2,1,0:T(2,128)(2,1)} %get-tuple-element.860, s32[]{:T(128)} %get-tuple-element.842), kind=kLoop, calls=%fused_computation.20.clone.1 | loop fusion | bytes 4194308 | tf_op jit(solution)/shard_map/while/body/jit(dynamic_index_in_dim)/dynamic_slice | solution.py:73
  34.0 3.9 %fusion.129 = (f32[64,2,8]{0,2,1:T(8,128)S(1)}, f32[2,4096,64,8]{1,2,3,0:T(8,128)S(1)}) fusion(pred[64,4096]{1,0:T(8,128)(4,1)S(1)} %broadcast_compare_fusion.2, bf16[64,2,8,128]{3,0,2,1:T(8,128)(2,1)S(1)} %get-tuple-element.861, bf16[1,4096,2,128]{3,2,1,0:T(2,128)(2,1)S(1)} %constant_dynamic-slice_fusion.4), kind=kOutput, calls=%fused_computation.5.clone.1 | convolution fusion | flops 1086323712 | bytes 19402752 | tf_op jit(solution)/shard_map/while/body/eval_jaxpr/qgrd,kgd->qgrk/dot_general | solution.py:58
  37.9 0.0 copy-start
  37.9 4.9 %fusion.131 = f32[64,2,8]{0,2,1:T(8,128)S(1)} fusion(f32[2,4096,64,8]{1,2,3,0:T(8,128)S(1)} %get-tuple-element.805, f32[64,2,8]{0,2,1:T(8,128)S(1)} %get-tuple-element.804, pred[64,4096]{1,0:T(8,128)(4,1)S(1)} %broadcast_compare_fusion.2), kind=kLoop, calls=%fused_computation.4.clone.1 | loop fusion | flops 16776192 | bytes 17047552 | tf_op jit(solution)/shard_map/while/body/eval_jaxpr/reduce_sum | solution.py:66
  42.8 0.8 copy-done
  43.6 3.2 %constant_dynamic-slice_fusion.5 = bf16[1,4096,2,128]{3,2,1,0:T(2,128)(2,1)S(1)} fusion(bf16[4,4096,2,128]{3,2,1,0:T(2,128)(2,1)} %get-tuple-element.862, s32[]{:T(128)} %get-tuple-element.842), kind=kLoop, calls=%fused_computation.19.clone.1 | loop fusion | bytes 4194308 | tf_op jit(solution)/shard_map/while/body/jit(dynamic_index_in_dim)/dynamic_slice | solution.py:73
  46.9 7.8 %fusion.130 = f32[64,2,8]{0,2,1:T(8,128)S(1)} fusion(f32[2,4096,64,8]{1,2,3,0:T(8,128)} %copy-done, f32[64,2,8]{0,2,1:T(8,128)S(1)} %get-tuple-element.804, pred[64,4096]{1,0:T(8,128)(4,1)S(1)} %broadcast_compare_fusion.2, bf16[1,4096,2,128]{3,2,1,0:T(2,128)(2,1)S(1)} %constant_dynamic-slice_fusion.5, f32[2,8,128]{2,1,0:T(8,128)S(1)} %bitcast.456), kind=kOutput, calls=%fused_computation.13.clone.1 | convolution fusion | flops 1090780160 | bytes 19152896 | tf_op jit(solution)/shard_map/while/body/eval_jaxpr/qgrk,kgd->qgrd/dot_general | solution.py:67
  54.7 0.7 dynamic_slice.114
  56.1 0.2 broadcast_compare_fusion.2
  56.3 3.3 %constant_dynamic-slice_fusion.4 = bf16[1,4096,2,128]{3,2,1,0:T(2,128)(2,1)S(1)} fusion(bf16[4,4096,2,128]{3,2,1,0:T(2,128)(2,1)} %get-tuple-element.860, s32[]{:T(128)} %get-tuple-element.842), kind=kLoop, calls=%fused_computation.20.clone.1 | loop fusion | bytes 4194308 | tf_op jit(solution)/shard_map/while/body/jit(dynamic_index_in_dim)/dynamic_slice | solution.py:73
  59.6 3.9 %fusion.129 = (f32[64,2,8]{0,2,1:T(8,128)S(1)}, f32[2,4096,64,8]{1,2,3,0:T(8,128)S(1)}) fusion(pred[64,4096]{1,0:T(8,128)(4,1)S(1)} %broadcast_compare_fusion.2, bf16[64,2,8,128]{3,0,2,1:T(8,128)(2,1)S(1)} %get-tuple-element.861, bf16[1,4096,2,128]{3,2,1,0:T(2,128)(2,1)S(1)} %constant_dynamic-slice_fusion.4), kind=kOutput, calls=%fused_computation.5.clone.1 | convolution fusion | flops 1086323712 | bytes 19402752 | tf_op jit(solution)/shard_map/while/body/eval_jaxpr/qgrd,kgd->qgrk/dot_general | solution.py:58
  63.5 0.0 copy-start
  63.5 4.9 %fusion.131 = f32[64,2,8]{0,2,1:T(8,128)S(1)} fusion(f32[2,4096,64,8]{1,2,3,0:T(8,128)S(1)} %get-tuple-element.805, f32[64,2,8]{0,2,1:T(8,128)S(1)} %get-tuple-element.804, pred[64,4096]{1,0:T(8,128)(4,1)S(1)} %broadcast_compare_fusion.2), kind=kLoop, calls=%fused_computation.4.clone.1 | loop fusion | flops 16776192 | bytes 17047552 | tf_op jit(solution)/shard_map/while/body/eval_jaxpr/reduce_sum | solution.py:66
  68.4 0.8 copy-done
  69.2 3.2 %constant_dynamic-slice_fusion.5 = bf16[1,4096,2,128]{3,2,1,0:T(2,128)(2,1)S(1)} fusion(bf16[4,4096,2,128]{3,2,1,0:T(2,128)(2,1)} %get-tuple-element.862, s32[]{:T(128)} %get-tuple-element.842), kind=kLoop, calls=%fused_computation.19.clone.1 | loop fusion | bytes 4194308 | tf_op jit(solution)/shard_map/while/body/jit(dynamic_index_in_dim)/dynamic_slice | solution.py:73
  72.5 7.8 %fusion.130 = f32[64,2,8]{0,2,1:T(8,128)S(1)} fusion(f32[2,4096,64,8]{1,2,3,0:T(8,128)} %copy-done, f32[64,2,8]{0,2,1:T(8,128)S(1)} %get-tuple-element.804, pred[64,4096]{1,0:T(8,128)(4,1)S(1)} %broadcast_compare_fusion.2, bf16[1,4096,2,128]{3,2,1,0:T(2,128)(2,1)S(1)} %constant_dynamic-slice_fusion.5, f32[2,8,128]{2,1,0:T(8,128)S(1)} %bitcast.456), kind=kOutput, calls=%fused_computation.13.clone.1 | convolution fusion | flops 1090780160 | bytes 19152896 | tf_op jit(solution)/shard_map/while/body/eval_jaxpr/qgrk,kgd->qgrd/dot_general | solution.py:67
  80.3 0.7 dynamic_slice.114
  81.7 0.2 broadcast_compare_fusion.2
  81.9 3.3 %constant_dynamic-slice_fusion.4 = bf16[1,4096,2,128]{3,2,1,0:T(2,128)(2,1)S(1)} fusion(bf16[4,4096,2,128]{3,2,1,0:T(2,128)(2,1)} %get-tuple-element.860, s32[]{:T(128)} %get-tuple-element.842), kind=kLoop, calls=%fused_computation.20.clone.1 | loop fusion | bytes 4194308 | tf_op jit(solution)/shard_map/while/body/jit(dynamic_index_in_dim)/dynamic_slice | solution.py:73
  85.2 3.9 %fusion.129 = (f32[64,2,8]{0,2,1:T(8,128)S(1)}, f32[2,4096,64,8]{1,2,3,0:T(8,128)S(1)}) fusion(pred[64,4096]{1,0:T(8,128)(4,1)S(1)} %broadcast_compare_fusion.2, bf16[64,2,8,128]{3,0,2,1:T(8,128)(2,1)S(1)} %get-tuple-element.861, bf16[1,4096,2,128]{3,2,1,0:T(2,128)(2,1)S(1)} %constant_dynamic-slice_fusion.4), kind=kOutput, calls=%fused_computation.5.clone.1 | convolution fusion | flops 1086323712 | bytes 19402752 | tf_op jit(solution)/shard_map/while/body/eval_jaxpr/qgrd,kgd->qgrk/dot_general | solution.py:58
  89.1 0.0 copy-start
  89.1 4.9 %fusion.131 = f32[64,2,8]{0,2,1:T(8,128)S(1)} fusion(f32[2,4096,64,8]{1,2,3,0:T(8,128)S(1)} %get-tuple-element.805, f32[64,2,8]{0,2,1:T(8,128)S(1)} %get-tuple-element.804, pred[64,4096]{1,0:T(8,128)(4,1)S(1)} %broadcast_compare_fusion.2), kind=kLoop, calls=%fused_computation.4.clone.1 | loop fusion | flops 16776192 | bytes 17047552 | tf_op jit(solution)/shard_map/while/body/eval_jaxpr/reduce_sum | solution.py:66
  94.0 0.8 copy-done
  94.8 3.2 %constant_dynamic-slice_fusion.5 = bf16[1,4096,2,128]{3,2,1,0:T(2,128)(2,1)S(1)} fusion(bf16[4,4096,2,128]{3,2,1,0:T(2,128)(2,1)} %get-tuple-element.862, s32[]{:T(128)} %get-tuple-element.842), kind=kLoop, calls=%fused_computation.19.clone.1 | loop fusion | bytes 4194308 | tf_op jit(solution)/shard_map/while/body/jit(dynamic_index_in_dim)/dynamic_slice | solution.py:73
  98.1 7.8 %fusion.130 = f32[64,2,8]{0,2,1:T(8,128)S(1)} fusion(f32[2,4096,64,8]{1,2,3,0:T(8,128)} %copy-done, f32[64,2,8]{0,2,1:T(8,128)S(1)} %get-tuple-element.804, pred[64,4096]{1,0:T(8,128)(4,1)S(1)} %broadcast_compare_fusion.2, bf16[1,4096,2,128]{3,2,1,0:T(2,128)(2,1)S(1)} %constant_dynamic-slice_fusion.5, f32[2,8,128]{2,1,0:T(8,128)S(1)} %bitcast.456), kind=kOutput, calls=%fused_computation.13.clone.1 | convolution fusion | flops 1090780160 | bytes 19152896 | tf_op jit(solution)/shard_map/while/body/eval_jaxpr/qgrk,kgd->qgrd/dot_general | solution.py:67
  105.9 0.7 dynamic_slice.114
  107.3 0.2 broadcast_compare_fusion.2
  107.5 3.3 %constant_dynamic-slice_fusion.4 = bf16[1,4096,2,128]{3,2,1,0:T(2,128)(2,1)S(1)} fusion(bf16[4,4096,2,128]{3,2,1,0:T(2,128)(2,1)} %get-tuple-element.860, s32[]{:T(128)} %get-tuple-element.842), kind=kLoop, calls=%fused_computation.20.clone.1 | loop fusion | bytes 4194308 | tf_op jit(solution)/shard_map/while/body/jit(dynamic_index_in_dim)/dynamic_slice | solution.py:73
  110.8 3.9 %fusion.129 = (f32[64,2,8]{0,2,1:T(8,128)S(1)}, f32[2,4096,64,8]{1,2,3,0:T(8,128)S(1)}) fusion(pred[64,4096]{1,0:T(8,128)(4,1)S(1)} %broadcast_compare_fusion.2, bf16[64,2,8,128]{3,0,2,1:T(8,128)(2,1)S(1)} %get-tuple-element.861, bf16[1,4096,2,128]{3,2,1,0:T(2,128)(2,1)S(1)} %constant_dynamic-slice_fusion.4), kind=kOutput, calls=%fused_computation.5.clone.1 | convolution fusion | flops 1086323712 | bytes 19402752 | tf_op jit(solution)/shard_map/while/body/eval_jaxpr/qgrd,kgd->qgrk/dot_general | solution.py:58
  114.7 0.0 copy-start
  114.7 4.9 %fusion.131 = f32[64,2,8]{0,2,1:T(8,128)S(1)} fusion(f32[2,4096,64,8]{1,2,3,0:T(8,128)S(1)} %get-tuple-element.805, f32[64,2,8]{0,2,1:T(8,128)S(1)} %get-tuple-element.804, pred[64,4096]{1,0:T(8,128)(4,1)S(1)} %broadcast_compare_fusion.2), kind=kLoop, calls=%fused_computation.4.clone.1 | loop fusion | flops 16776192 | bytes 17047552 | tf_op jit(solution)/shard_map/while/body/eval_jaxpr/reduce_sum | solution.py:66
  119.6 0.8 copy-done
  120.4 3.2 %constant_dynamic-slice_fusion.5 = bf16[1,4096,2,128]{3,2,1,0:T(2,128)(2,1)S(1)} fusion(bf16[4,4096,2,128]{3,2,1,0:T(2,128)(2,1)} %get-tuple-element.862, s32[]{:T(128)} %get-tuple-element.842), kind=kLoop, calls=%fused_computation.19.clone.1 | loop fusion | bytes 4194308 | tf_op jit(solution)/shard_map/while/body/jit(dynamic_index_in_dim)/dynamic_slice | solution.py:73
  123.6 7.8 %fusion.130 = f32[64,2,8]{0,2,1:T(8,128)S(1)} fusion(f32[2,4096,64,8]{1,2,3,0:T(8,128)} %copy-done, f32[64,2,8]{0,2,1:T(8,128)S(1)} %get-tuple-element.804, pred[64,4096]{1,0:T(8,128)(4,1)S(1)} %broadcast_compare_fusion.2, bf16[1,4096,2,128]{3,2,1,0:T(2,128)(2,1)S(1)} %constant_dynamic-slice_fusion.5, f32[2,8,128]{2,1,0:T(8,128)S(1)} %bitcast.456), kind=kOutput, calls=%fused_computation.13.clone.1 | convolution fusion | flops 1090780160 | bytes 19152896 | tf_op jit(solution)/shard_map/while/body/eval_jaxpr/qgrk,kgd->qgrd/dot_general | solution.py:67
  131.5 30.5 %all_gather.7 = f32[8,64,2,8]{1,3,2,0:T(8,128)S(1)} all-gather(f32[1,64,2,8]{1,3,2,0:T(8,128)S(1)} %multiply_add_fusion.1), channel_id=1, replica_groups=mesh['keys'=8,'heads'=4] {'keys'}, dimensions={0}, use_global_device_ids=true | all-gather | bytes 36864 | tf_op jit(solution)/shard_map/all_gather | solution.py:14
  162.1 30.5 %all_gather.6 = f32[8,64,2,8]{1,3,2,0:T(8,128)S(1)} all-gather(f32[1,64,2,8]{1,3,2,0:T(8,128)S(1)} %get-tuple-element.640), channel_id=1, replica_groups=mesh['keys'=8,'heads'=4] {'keys'}, dimensions={0}, use_global_device_ids=true | all-gather | bytes 36864 | tf_op jit(solution)/shard_map/all_gather | solution.py:14
  192.6 30.5 %all_gather.8 = f32[8,64,2,8]{1,3,2,0:T(8,128)S(1)} all-gather(f32[1,64,2,8]{1,3,2,0:T(8,128)S(1)} %get-tuple-element.639), channel_id=1, replica_groups=mesh['keys'=8,'heads'=4] {'keys'}, dimensions={0}, use_global_device_ids=true | all-gather | bytes 36864 | tf_op jit(solution)/shard_map/all_gather | solution.py:14
  223.1 0.4 while.56
  223.5 0.4 while.57
  224.0 0.1 fusion.115
  224.1 0.1 fusion.113
  224.1 0.1 fusion.114
  224.2 5.7 %psum.22 = f32[64,4]{0,1:T(4,128)S(1)} all-reduce(f32[64,4]{0,1:T(4,128)S(1)} %pad_maximum_fusion), channel_id=1, replica_groups=mesh['keys'=8,'heads'=4] {'heads'}, use_global_device_ids=true, to_apply=%region_14.15 | all-reduce | flops 256 | bytes 2048 | tf_op jit(solution)/shard_map/psum | solution.py:98
  229.8 0.0 copy-start.2
  229.9 0.0 copy-done.1
  229.9 0.1 select_reduce_fusion
  229.9 18.0 %psum.23 = f32[64,16]{0,1:T(8,128)} all-reduce(f32[64,16]{0,1:T(8,128)S(1)} %select_reduce_fusion), channel_id=1, replica_groups=mesh['keys'=8,'heads'=4] {'keys'}, use_global_device_ids=true, to_apply=%region_16.17 | all-reduce | flops 1024 | bytes 8192 | tf_op jit(solution)/shard_map/psum | solution.py:102
  247.9 0.0 copy-done.2
  (47 shorter events, 0.5 us)
Async XLA Ops:
  29.1 200.7 %copy-start.1 = (s32[64,16]{0,1:T(8,128)S(1)}, s32[64,16]{0,1:T(8,128)}, u32[]{:S(2)}) copy-start(s32[64,16]{0,1:T(8,128)} %param.17) | copy-start | bytes 12292
  37.9 5.7 %copy-start = (f32[2,4096,64,8]{1,2,3,0:T(8,128)}, f32[2,4096,64,8]{1,2,3,0:T(8,128)S(1)}, u32[]{:S(2)}) copy-start(f32[2,4096,64,8]{1,2,3,0:T(8,128)S(1)} %get-tuple-element.805) | copy-start | bytes 50331652 | tf_op jit(solution)/shard_map/while
  63.5 5.7 %copy-start = (f32[2,4096,64,8]{1,2,3,0:T(8,128)}, f32[2,4096,64,8]{1,2,3,0:T(8,128)S(1)}, u32[]{:S(2)}) copy-start(f32[2,4096,64,8]{1,2,3,0:T(8,128)S(1)} %get-tuple-element.805) | copy-start | bytes 50331652 | tf_op jit(solution)/shard_map/while
  89.1 5.7 %copy-start = (f32[2,4096,64,8]{1,2,3,0:T(8,128)}, f32[2,4096,64,8]{1,2,3,0:T(8,128)S(1)}, u32[]{:S(2)}) copy-start(f32[2,4096,64,8]{1,2,3,0:T(8,128)S(1)} %get-tuple-element.805) | copy-start | bytes 50331652 | tf_op jit(solution)/shard_map/while
  114.7 5.7 %copy-start = (f32[2,4096,64,8]{1,2,3,0:T(8,128)}, f32[2,4096,64,8]{1,2,3,0:T(8,128)S(1)}, u32[]{:S(2)}) copy-start(f32[2,4096,64,8]{1,2,3,0:T(8,128)S(1)} %get-tuple-element.805) | copy-start | bytes 50331652 | tf_op jit(solution)/shard_map/while
  229.8 18.0 %copy-start.2 = (f32[64,4]{0,1:T(4,128)}, f32[64,4]{0,1:T(4,128)S(1)}, u32[]{:S(2)}) copy-start(f32[64,4]{0,1:T(4,128)S(1)} %psum.22) | copy-start | bytes 3076
where the time goes:
time: 249 us; the launch traced here: 248 us
  blocking collectives  139 us (56%)
  matrix products  50.2 us (20%)
  local copies, waits for them, and re-layouts  33.7 us (14%)
  other arithmetic  21.1 us (8%)
  loops' own time  3.64 us (1%)
    all_gather x3, blocking collectives, entering(): everything = jax.tree.map(lambda part: lax.all_gather(part, axis), x)  91.6 us
    dot_general x4, matrix products, block_state(): jnp.einsum('qgrk,kgd->qgrd', weights.astype(jnp.bfloat16), vblk, preferre...  31.1 us
    dynamic_slice x12, local copies, waits for them, and re-layouts, body(): lax.map(block_state, (key_blocks, value_blocks, jnp.arange(nblk, dtype=jn...  28.6 us
    psum x1, blocking collectives, body(): lax.psum(jnp.dot(out_weight, probe, preferred_element_type=jnp.float32),...  23.4 us
    reduce_sum x4, other arithmetic, block_state(): total = jnp.sum(weights, axis=-1)  19.6 us
    psum x1, blocking collectives, body(): picked = lax.psum(local_pick, 'keys')  18 us
    dot_general x4, matrix products, block_state(): jnp.einsum('qgrd,kgd->qgrk', grouped, kblk, preferred_element_type=jnp.fl...  15.7 us
    psum x1, blocking collectives, body(): readout = lax.psum(partial_read, 'heads')  5.67 us

commit v1 on v0

v1 whole, which is shorter than its diff:
```python
import functools
import math

import jax
import jax.numpy as jnp
from jax import lax
from jax.experimental import pallas as pl
from jax.experimental.pallas import tpu as pltpu
from jax.sharding import PartitionSpec as P

BLOCK = 4096
NEG = -1e30
LANES = 128
CHUNK = 512
MESH = pl.DeviceIdType.MESH


def combine(first, second):
    m1, s1, o1 = first
    m2, s2, o2 = second
    top = jnp.maximum(m1, m2)
    a = jnp.exp(m1 - top)
    b = jnp.exp(m2 - top)
    return (top, s1 * a + s2 * b, o1 * a + o2 * b)


def exchange(size, axis, src, held, send, recv, start=True):
    me = lax.axis_index(axis)
    out = []
    for k in range(1, size):
        there = lax.rem(me + k, size)
        here = lax.rem(me + size - k, size)
        put = pltpu.make_async_remote_copy(src, held.at[me], send.at[k], recv.at[k], device_id={axis: there}, device_id_type=MESH)
        get = pltpu.make_async_remote_copy(src, held.at[here], send.at[k], recv.at[k], device_id={axis: there}, device_id_type=MESH)
        if start:
            put.start()
        out.append((put, get))
    return out


def finish(copies):
    for put, get in copies:
        get.wait_recv()
    for put, get in copies:
        put.wait_send()


def attend(lanes, hn, nblk, kvh, group, q_ref, k_ref, v_ref, w_ref, x_ref, all_ref,
           q2, pm, rel, sc, m_rep, m_run, s_run, o_all, cols, flip, st, tot, part, own,
           dirs, tots, reads, held, d_send, d_recv, t_send, t_recv, r_send, r_recv, g_send, g_recv):
    i = pl.program_id(0)
    nq, hq, hd = q_ref.shape
    rows = nq * group
    nchunk = k_ref.shape[0] // CHUNK
    tiles = CHUNK // LANES
    flat = rows // LANES
    scale = hd ** -0.5 * math.log2(math.e)
    device = lax.axis_index("keys")
    mine = lax.axis_index("heads")
    barrier = pltpu.get_barrier_semaphore()

    @pl.when(i == 0)
    def _():
        for k in range(1, lanes):
            pl.semaphore_signal(barrier, inc=1, device_id={"keys": lax.rem(device + k, lanes)}, device_id_type=MESH)
        for k in range(1, hn):
            pl.semaphore_signal(barrier, inc=1, device_id={"heads": lax.rem(mine + k, hn)}, device_id_type=MESH)
        q = q_ref[...].astype(jnp.float32)
        for h in range(kvh):
            piece = q[:, h * group:(h + 1) * group, :].reshape(rows, hd)
            q2[:, h * hd:(h + 1) * hd] = piece.astype(jnp.bfloat16)
        row = lax.broadcasted_iota(jnp.int32, (CHUNK, hd), 0)
        for h in range(kvh):
            pm[h] = jnp.where(lax.rem(row, kvh) == h, 1.0, 0.0).astype(jnp.bfloat16)
        r = lax.broadcasted_iota(jnp.int32, (rows, LANES), 0)
        c = lax.broadcasted_iota(jnp.int32, (rows, LANES), 1)
        rel[...] = (c // kvh + (CHUNK - LANES) // kvh) - r // group
        cols[...] = jnp.zeros_like(cols)

    def spread(ref, j):
        x = ref[pl.ds(pl.multiple_of(j * CHUNK, CHUNK), CHUNK), :]
        return jnp.concatenate([x * pm[h] for h in range(kvh)], axis=1)

    def score(j):
        s = lax.dot_general(q2[...], spread(k_ref, j), (((1,), (1,)), ((), ())), preferred_element_type=jnp.float32)
        base = (device * nblk + i) * BLOCK + j * (CHUNK // kvh)
        first = lanes * nblk * BLOCK - nq
        last = jnp.where(rel[...] <= first - base, s[:, CHUNK - LANES:], NEG)
        parts = [s[:, t * LANES:(t + 1) * LANES] for t in range(tiles - 1)] + [last]
        top = m_run[...]
        for t in range(tiles):
            sc[j, :, t * LANES:(t + 1) * LANES] = parts[t]
            top = jnp.maximum(top, parts[t])
        m_run[...] = top

    def weigh(j):
        m = m_rep[...]
        total = s_run[...]
        parts = []
        for t in range(tiles):
            p = jnp.exp2((sc[j, :, t * LANES:(t + 1) * LANES] - m) * scale)
            total = total + p
            parts.append(p.astype(jnp.bfloat16))
        s_run[...] = total
        o_all[i] += jnp.dot(jnp.concatenate(parts, axis=1), spread(v_ref, j), preferred_element_type=jnp.float32)

    lane = lax.broadcasted_iota(jnp.int32, (rows, LANES), 1)
    states = nblk * kvh
    some = lax.dot_general(jnp.broadcast_to(x_ref[...], (16, x_ref.shape[1])), w_ref[...], (((1,), (1,)), ((), ())),
                           preferred_element_type=jnp.float32)
    count = hq // nblk
    for t in range(count):
        part[pl.ds(i * count + t, 1), :] = some[0:1, t * hd:(t + 1) * hd]

    @pl.when(i == nblk - 1)
    def _():
        pl.semaphore_wait(barrier, lanes + hn - 2)
        exchange(lanes, "keys", part, dirs, d_send, d_recv, True)
        dirs[device] = part[...]

    m_run[...] = jnp.full_like(m_run, 2 * NEG)

    @pl.loop(0, nchunk)
    def _(j):
        score(j)

    run = m_run[...]
    out = jnp.zeros_like(run)
    acc = cols[...]
    for h in range(kvh):
        top = jnp.max(jnp.where(lax.rem(lane, kvh) == h, run, 2 * NEG), axis=1, keepdims=True)
        out = jnp.where(lax.rem(lane, kvh) == h, top, out)
        acc = jnp.where(lane == i * kvh + h, top * hd ** -0.5, acc)
    m_rep[...] = out
    s_run[...] = jnp.zeros_like(s_run)
    o_all[i] = jnp.zeros(o_all.shape[1:], jnp.float32)

    @pl.loop(0, nchunk)
    def _(j):
        weigh(j)

    for h in range(kvh):
        total = jnp.sum(jnp.where(lax.rem(lane, kvh) == h, s_run[...], 0.0), axis=1, keepdims=True)
        acc = jnp.where(lane == states + i * kvh + h, total, acc)
    cols[...] = acc

    @pl.when(i == nblk - 1)
    def _():
        finish(exchange(lanes, "keys", part, dirs, d_send, d_recv, False))
        direction = dirs[0]
        for k in range(1, lanes):
            direction = direction + dirs[k]
        acc = cols[...]
        for b in range(nblk):
            for h in range(kvh):
                o = o_all[b, :, h * hd:(h + 1) * hd].reshape(nq, group, hd) * direction[h * group:(h + 1) * group, :][None]
                o = jnp.sum(o.reshape(rows, hd), axis=1, keepdims=True)
                acc = jnp.where(lane == 2 * states + b * kvh + h, o, acc)
        flip[...] = acc.T
        for kind in range(3):
            for b in range(nblk):
                for h in range(kvh):
                    at = kind * states + b * kvh + h
                    for t in range(flat):
                        st[b, kind, h * flat + t:h * flat + t + 1, :] = flip[at:at + 1, t * LANES:(t + 1) * LANES]
        local = [tuple(st[b, kind] for kind in range(3)) for b in range(nblk)]
        whole = functools.reduce(combine, local)
        for kind in range(3):
            tot[kind] = whole[kind]
        copies = exchange(lanes, "keys", tot, tots, t_send, t_recv)
        shape = local[0][0].shape
        empty = (jnp.full(shape, NEG, jnp.float32), jnp.zeros(shape, jnp.float32), jnp.zeros(shape, jnp.float32))
        for kind in range(3):
            tots[device, kind] = empty[kind]
        finish(copies)
        outer = functools.reduce(combine, [tuple(tots[k, kind] for kind in range(3)) for k in range(lanes)])
        slim = lax.broadcasted_iota(jnp.int32, shape, 1)
        packed = jnp.zeros(shape, jnp.float32)
        for b in range(nblk):
            _, s, o = functools.reduce(combine, [local[c] for c in range(nblk) if c != b], outer)
            x = o / s
            step = 1
            while step < group:
                x = x + pltpu.roll(x, LANES - step, 1)
                step *= 2
            if b:
                x = pltpu.roll(x, b, 1)
            packed = jnp.where(lax.rem(slim, group) == b, x, packed)
        own[...] = functools.reduce(jnp.add, [packed[h * flat:(h + 1) * flat] for h in range(kvh)])
        copies = exchange(hn, "heads", own, reads, r_send, r_recv)
        reads[mine] = own[...]
        finish(copies)
        part[0:flat, :] = functools.reduce(jnp.add, [reads[k] for k in range(hn)])
        copies = exchange(lanes, "keys", part.at[pl.ds(0, flat)], held, g_send, g_recv)
        held[device] = part[0:flat, :]
        finish(copies)
        all_ref[...] = held[...]


def body(queries, keys, values, out_weight, probe, knocked):
    nq, hq, hd = queries.shape
    kvh = keys.shape[1]
    group = hq // kvh
    nblk = keys.shape[0] // BLOCK
    lanes = lax.axis_size("keys")
    hn = lax.axis_size("heads")
    device = lax.axis_index("keys")
    rows = nq * group
    flat = rows // LANES
    wide = BLOCK * kvh
    f32 = jnp.float32
    dma = pltpu.SemaphoreType.DMA
    every = pl.pallas_call(
        functools.partial(attend, lanes, hn, nblk, kvh, group),
        grid=(nblk,),
        in_specs=[
            pl.BlockSpec((nq, hq, hd), lambda i: (0, 0, 0)),
            pl.BlockSpec((wide, hd), lambda i: (i, 0)),
            pl.BlockSpec((wide, hd), lambda i: (i, 0)),
            pl.BlockSpec((hq * hd // nblk, out_weight.shape[1]), lambda i: (i, 0)),
            pl.BlockSpec((1, out_weight.shape[1]), lambda i: (0, 0)),
        ],
        out_specs=pl.BlockSpec(memory_space=pltpu.VMEM),
        out_shape=jax.ShapeDtypeStruct((lanes, flat, LANES), f32),
        scratch_shapes=[
            pltpu.VMEM((rows, kvh * hd), jnp.bfloat16),
            pltpu.VMEM((kvh, CHUNK, hd), jnp.bfloat16),
            pltpu.VMEM((rows, LANES), jnp.int32),
            pltpu.VMEM((wide // CHUNK, rows, CHUNK), f32),
            pltpu.VMEM((rows, LANES), f32),
            pltpu.VMEM((rows, LANES), f32),
            pltpu.VMEM((rows, LANES), f32),
            pltpu.VMEM((nblk, rows, kvh * hd), f32),
            pltpu.VMEM((rows, LANES), f32),
            pltpu.VMEM((LANES, rows), f32),
            pltpu.VMEM((nblk, 3, kvh * flat, LANES), f32),
            pltpu.VMEM((3, kvh * flat, LANES), f32),
            pltpu.VMEM((hq, hd), f32),
            pltpu.VMEM((flat, LANES), f32),
            pltpu.VMEM((lanes, hq, hd), f32),
            pltpu.VMEM((lanes, 3, kvh * flat, LANES), f32),
            pltpu.VMEM((hn, flat, LANES), f32),
            pltpu.VMEM((lanes, flat, LANES), f32),
            dma((lanes,)), dma((lanes,)), dma((lanes,)), dma((lanes,)),
            dma((hn,)), dma((hn,)), dma((lanes,)), dma((lanes,)),
        ],
        compiler_params=pltpu.CompilerParams(collective_id=0, has_side_effects=True, vmem_limit_bytes=60 * 2 ** 20),
    )(queries, keys.reshape(-1, hd), values.reshape(-1, hd), out_weight, probe.reshape(1, -1))
    every = every.reshape(lanes, nq, group)[:, :, :nblk]
    readout = lax.dynamic_index_in_dim(every, device, 0, False)
    table = jnp.swapaxes(every, 0, 1).reshape(nq, lanes * nblk)
    ids = jnp.arange(lanes * nblk, dtype=jnp.int32)
    picked = jnp.sum(jnp.where(knocked[:, :, None] == ids, table[:, None, :], 0.0), axis=-1)
    return (readout, picked)


def solution(mesh):
    in_specs = (
        P(None, "heads", None),
        P("keys", "heads", None),
        P("keys", "heads", None),
        P("heads", "keys"),
        P("keys"),
        P(),
    )
    out_specs = (P(None, "keys"), P())
    return jax.shard_map(body, mesh=mesh, in_specs=in_specs, out_specs=out_specs, check_vma=False)
```

time: 249 us -> 73.1 us (0.29)
  blocking collectives: 139 us -> 0 us
  Pallas kernels: 0 us -> 68.6 us
  matrix products: 50.2 us -> 0 us
  local copies, waits for them, and re-layouts: 33.7 us -> 3 us
  other arithmetic: 21.1 us -> 0.66 us
  loops' own time: 3.64 us -> 0 us
    all_gather x3 -> x0, blocking collectives: 91.6 us -> none  [entering(): everything = jax.tree.map(lambda part: lax.all_gather(part, axis), x)]
    pallas_call x0 -> x1, Pallas kernels: none -> 68.6 us  [body(): pl.pallas_call(functools.partial(attend, lanes, hn, nblk, kvh, group), gr...]
    dot_general x9 -> x0, matrix products: 50.2 us -> none  [the longest x4 31.1 us: block_state(): jnp.einsum('qgrk,kgd->qgrd', weights.astype(jnp.bfloat16), vblk, preferre...]
    psum x3 -> x0, blocking collectives: 47 us -> none  [the longest x1 23.4 us: body(): lax.psum(jnp.dot(out_weight, probe, preferred_element_type=jnp.float32),...]
    dynamic_slice x12 -> x2, local copies, waits for them, and re-layouts: 28.6 us -> 0.66 us  [body(): readout = lax.dynamic_index_in_dim(every, device, 0, False)]
    reduce_sum x9 -> x1, other arithmetic: 19.9 us -> 0.66 us  [body(): jnp.sum(jnp.where(knocked[:, :, None] == ids, table[:, None, :], 0.0), ax...]
    another operation x3 -> x0, loops' own time: 3.64 us -> none  [the longest x1 3.15 us: body(): lax.map(block_state, (key_blocks, value_blocks, jnp.arange(nblk, dtype=jn...]
    while x8 -> x0, local copies, waits for them, and re-layouts: 3.24 us -> none
where the time goes in v1:
time: 73.1 us; the launch traced here: 72.9 us
  Pallas kernels  68.6 us (94%)
  local copies, waits for them, and re-layouts  3 us (4%)
    pallas_call x1, Pallas kernels, body(): pl.pallas_call(functools.partial(attend, lanes, hn, nblk, kvh, group), gr...  68.6 us

profile of v1, /device:TPU:0, one launch (start us, length us, event | category | flops | bytes accessed | tf_op | source)
XLA Modules:
  0.0 72.9 jit_solution(10678917295254029641)
XLA Ops:
  0.6 1.3 %reshape.20.x_ref = bf16[1,1024]{1,0:T(2,128)(2,1)} reshape(bf16[1024]{0:T(1024)(128)(2,1)} %param.10) | data formatting | bytes 4096 | tf_op jit(solution)/shard_map/reshape | solution.py:248
  1.9 0.0 copy-start
  1.9 68.6 %shard_map.77 = f32[8,4,128]{2,1,0:T(4,128)} custom-call(bf16[64,16,128]{2,1,0:T(8,128)(2,1)} %q_ref.1, bf16[32768,128]{1,0:T(8,128)(2,1)} %bitcast.6, bf16[32768,128]{1,0:T(8,128)(2,1)} %bitcast.7, bf16[2048,1024]{1,0:T(8,128)(2,1)} %w_ref.1, bf16[1,1024]{1,0:T(2,128)(2,1)} %reshape.20.x_ref), custom_call_target="tpu_custom_call" | custom-call | tf_op jit(solution)/shard_map/pallas_call | solution.py:213
  70.5 0.9 %reshape.21 = f32[8,64,8]{2,1,0:T(8,128)S(1)} reshape(f32[8,4,128]{2,1,0:T(4,128)} %shard_map.77) | data formatting | bytes 32768 | tf_op jit(solution)/shard_map/reshape | solution.py:249
  71.4 0.1 slice_bitcast_fusion
  71.4 0.7 copy.17
  72.1 0.1 copy.18
  72.2 0.0 copy-done
  72.2 0.7 select_reduce_fusion
  (1 shorter events, 0.0 us)
Async XLA Ops:
  1.9 70.3 %copy-start = (s32[64,16]{0,1:T(8,128)S(1)}, s32[64,16]{0,1:T(8,128)}, u32[]{:S(2)}) copy-start(s32[64,16]{0,1:T(8,128)} %param.11) | copy-start | bytes 12292

commit v2 on v1

--- a/solution.py
+++ b/solution.py
@@ -11,7 +11,7 @@
 BLOCK = 4096
 NEG = -1e30
 LANES = 128
-CHUNK = 512
+CHUNK = 2048
 MESH = pl.DeviceIdType.MESH
 
 

time: 73.1 us -> 56.2 us (0.77)
  Pallas kernels: 68.6 us -> 51.6 us
    pallas_call x1, Pallas kernels: 68.6 us -> 51.6 us  [body(): pl.pallas_call(functools.partial(attend, lanes, hn, nblk, kvh, group), gr...]
where the time goes in v2:
time: 56.2 us; the launch traced here: 55.9 us
  Pallas kernels  51.6 us (92%)
  local copies, waits for them, and re-layouts  3 us (5%)
  between operations  0.67 us (1%)
  other arithmetic  0.66 us (1%)
    pallas_call x1, Pallas kernels, body(): pl.pallas_call(functools.partial(attend, lanes, hn, nblk, kvh, group), gr...  51.6 us
    reshape x1, local copies, waits for them, and re-layouts, body(): probe.reshape(1, -1)  1.28 us

profile of v2, /device:TPU:0, one launch (start us, length us, event | category | flops | bytes accessed | tf_op | source)
XLA Modules:
  0.0 55.9 jit_solution(10029675856371856980)
XLA Ops:
  0.6 1.3 %reshape.20.x_ref = bf16[1,1024]{1,0:T(2,128)(2,1)} reshape(bf16[1024]{0:T(1024)(128)(2,1)} %param.10) | data formatting | bytes 4096 | tf_op jit(solution)/shard_map/reshape | solution.py:248
  1.9 0.0 copy-start
  1.9 51.6 %shard_map.77 = f32[8,4,128]{2,1,0:T(4,128)} custom-call(bf16[64,16,128]{2,1,0:T(8,128)(2,1)} %q_ref.1, bf16[32768,128]{1,0:T(8,128)(2,1)} %bitcast.6, bf16[32768,128]{1,0:T(8,128)(2,1)} %bitcast.7, bf16[2048,1024]{1,0:T(8,128)(2,1)} %w_ref.1, bf16[1,1024]{1,0:T(2,128)(2,1)} %reshape.20.x_ref), custom_call_target="tpu_custom_call" | custom-call | tf_op jit(solution)/shard_map/pallas_call | solution.py:213
  53.5 0.9 %reshape.21 = f32[8,64,8]{2,1,0:T(8,128)S(1)} reshape(f32[8,4,128]{2,1,0:T(4,128)} %shard_map.77) | data formatting | bytes 32768 | tf_op jit(solution)/shard_map/reshape | solution.py:249
  54.4 0.1 slice_bitcast_fusion
  54.5 0.7 %copy.17 = f32[1,64,4]{1,2,0:T(4,128)} copy(f32[1,64,4]{2,1,0:T(8,128)S(1)} %constant_dynamic-slice_fusion) | data formatting | bytes 2048 | tf_op jit(solution)/shard_map/jit(dynamic_index_in_dim)/dynamic_slice | solution.py:250
  55.2 0.1 copy.18
  55.3 0.0 copy-done
  55.3 0.7 %select_reduce_fusion = f32[64,16]{0,1:T(8,128)} fusion(f32[64,32]{0,1:T(8,128)S(1)} %bitcast.8, s32[64,16]{0,1:T(8,128)S(1)} %copy-done), kind=kLoop, calls=%fused_computation | loop fusion | flops 97280 | bytes 16384 | tf_op jit(solution)/shard_map/reduce_sum | solution.py:253
  (1 shorter events, 0.0 us)
Async XLA Ops:
  1.9 53.4 %copy-start = (s32[64,16]{0,1:T(8,128)S(1)}, s32[64,16]{0,1:T(8,128)}, u32[]{:S(2)}) copy-start(s32[64,16]{0,1:T(8,128)} %param.11) | copy-start | bytes 12292
